TPU v7x, 32 devices: a whole 2x2x4 slice. The times are simulated.
32 devices in a mesh: wide: 8 (over z, x), narrow: 4 (over y, core).
Axes of the slice: x: 2, y: 2, z: 4, core: 2. Of those that a mesh axis runs over, the one named last changes fastest.
Arguments:
- field: float32 [4, 512, 64, 512], P(None, 'narrow', 'wide'), may hold values from -200 to 200, as said below
- start: float32 [512, 128], replicated, may hold values from -6 to 6
Outputs:
- basis: float32 [512, 128], replicated
- core: float32 [128, 4, 64, 512], P('narrow', None, 'wide')
Inputs may be any that keep to these rules, and one draw needn't show every extreme that they name: `field`: every entry is finite; different x rows and species have different scales.
All inputs are finite; a program needn't handle non-finite values.
Results may differ from a plain program's by a relative error of at most 0.0003.
Values sent between devices are 32-bit elements; how exact they have to be, the bound alone decides.
A program may use at most 64 MiB of HBM per device.

v0:
```python
import jax
import jax.numpy as jnp
from jax import lax
from jax.sharding import PartitionSpec as P

ITERS = 3


def upper_pairs():
    return [(first, second) for first in range(4) for second in range(4) if first <= second]


def pack_upper(matrix):
    width = matrix.shape[0] // 4
    tiles = matrix.reshape(4, width, 4, width)
    return jnp.stack([tiles[first, :, second, :] for first, second in upper_pairs()], axis=0)


def unpack_upper(packed):
    where = {}
    for place, pair in enumerate(upper_pairs()):
        where[pair] = place
    rows_out = []
    for first in range(4):
        blocks = []
        for second in range(4):
            if first <= second:
                blocks.append(packed[where[first, second]])
            else:
                blocks.append(packed[where[second, first]].T)
        rows_out.append(jnp.concatenate(blocks, axis=1))
    return jnp.concatenate(rows_out, axis=0)


def local(field, start):
    spec_count, rows_local, cols_y, cells_z = field.shape
    groups = lax.axis_size("narrow")
    devices = lax.axis_size("wide") * groups
    regrouped = lax.all_to_all(field, "narrow", split_axis=2, concat_axis=1, tiled=True)
    partial_gram = jnp.einsum(
        "sxyz,swyz->xw",
        regrouped,
        regrouped,
        preferred_element_type=jnp.float32,
        precision=lax.Precision.HIGHEST,
    )
    columns = spec_count * regrouped.shape[2] * cells_z * devices
    summed = unpack_upper(lax.psum(pack_upper(partial_gram), ("wide", "narrow")))
    gram = summed / columns
    basis = start
    for step in range(ITERS):
        product = jnp.dot(
            gram, basis, preferred_element_type=jnp.float32, precision=lax.Precision.HIGHEST
        )
        cross = jnp.dot(
            product.T, product, preferred_element_type=jnp.float32, precision=lax.Precision.HIGHEST
        )
        lower = jnp.linalg.cholesky(cross)
        basis = jax.scipy.linalg.solve_triangular(lower, product.T, lower=True).T
    projected = jnp.einsum(
        "xr,sxyz->rsyz",
        basis,
        regrouped,
        preferred_element_type=jnp.float32,
        precision=lax.Precision.HIGHEST,
    )
    core = lax.all_to_all(projected, "narrow", split_axis=0, concat_axis=2, tiled=True)
    return (basis, core)


def solution(mesh):
    return jax.shard_map(
        local,
        mesh=mesh,
        in_specs=(P(None, "narrow", "wide", None), P()),
        out_specs=(P(), P("narrow", None, "wide", None)),
        check_vma=False,
    )
```

profile of v0, /device:TPU:0, one launch (start us, length us, event | category | flops | bytes accessed | tf_op | source)
XLA Modules:
  0.0 389.9 jit_solution(4721680181681200089)
XLA Ops:
  7.2 8.3 %copy.32 = f32[4,128,8,512]{3,1,0,2:T(8,128)S(1)} copy(f32[4,128,8,512]{3,2,1,0:T(8,128)} %param.5) | data formatting | bytes 16777216 | tf_op args[0]
  15.5 97.1 %all_to_all.36 = f32[4,128,8,512]{3,1,0,2:T(8,128)S(1)} all-to-all(f32[4,128,8,512]{3,1,0,2:T(8,128)S(1)} %copy.32), channel_id=1, replica_groups=mesh['wide'=8,'narrow'=4] {'narrow'}, dimensions={2} | all-to-all | bytes 16777216 | tf_op jit(solution)/shard_map/all_to_all | solution.py:39
  112.6 15.4 %fusion = f32[4,128,4,128,1,1]{3,1,5,2,0,4:T(8,128)S(1)} fusion(f32[4,128,4,2,512,1]{4,1,2,3,0,5:T(8,128)S(1)} %bitcast.157), kind=kOutput, calls=%fused_computation | convolution fusion | flops 12884901888 | bytes 9437184 | tf_op jit(solution)/shard_map/sxyz,swyz->xw/dot_general | solution.py:40
  128.3 0.8 copy-done.2
  129.2 8.2 %copy.33 = f32[4,128,4,2,512]{4,1,2,3,0:T(8,128)} copy(f32[4,128,4,2,512]{4,1,0,3,2:T(8,128)} %bitcast.158) | data formatting | bytes 16777216 | tf_op jit(solution)/shard_map/all_to_all | solution.py:39
  137.4 122.1 %all-reduce.2.cloned.1.call-done = f32[10,128,128]{2,1,0:T(8,128)} async-done(((f32[10,128,128]{2,1,0:T(8,128)}), f32[10,128,128]{2,1,0:T(8,128)}) %all-reduce.2.cloned.1.call-update) | async-done | bytes 655376 | tf_op jit(solution)/shard_map/psum | solution.py:48
  259.5 1.2 slice_bitcast_fusion.2
  261.5 1.0 fusion.34
  262.5 0.6 fusion.35
  263.2 11.7 %cholesky.59 = f32[128,128]{1,0:T(8,128)S(1)} custom-call(f32[128,128]{1,0:T(8,128)S(1)} %fusion.29), custom_call_target="Cholesky" | custom-call | tf_op jit(solution)/shard_map/jit(cholesky)/cholesky | solution.py:58
  275.0 0.6 compare_reduce_fusion.2
  275.6 0.7 fusion.11
  276.3 9.8 %custom-call.7 = f32[1,128,128]{1,2,0:T(8,128)S(1)} custom-call(f32[1,128,128]{2,1,0:T(8,128)S(1)} %fusion.11), custom_call_target="InvertDiagBlocksLowerTriangular" | custom-call | tf_op jit(solution)/shard_map/jit(_solve_triangular)/triangular_solve | solution.py:59
  286.5 1.0 fusion.36
  287.5 0.6 fusion.37
  288.2 11.9 %cholesky.70 = f32[128,128]{1,0:T(8,128)S(1)} custom-call(f32[128,128]{1,0:T(8,128)S(1)} %fusion.27), custom_call_target="Cholesky" | custom-call | tf_op jit(solution)/shard_map/jit(cholesky)/cholesky | solution.py:58
  300.2 0.6 compare_reduce_fusion.1
  300.8 0.7 fusion.12
  301.5 9.8 %custom-call.8 = f32[1,128,128]{1,2,0:T(8,128)S(1)} custom-call(f32[1,128,128]{2,1,0:T(8,128)S(1)} %fusion.12), custom_call_target="InvertDiagBlocksLowerTriangular" | custom-call | tf_op jit(solution)/shard_map/jit(_solve_triangular)/triangular_solve | solution.py:59
  311.7 1.0 fusion.38
  312.7 0.6 fusion.39
  313.4 11.7 %cholesky.81 = f32[128,128]{1,0:T(8,128)S(1)} custom-call(f32[128,128]{1,0:T(8,128)S(1)} %fusion.25), custom_call_target="Cholesky" | custom-call | tf_op jit(solution)/shard_map/jit(cholesky)/cholesky | solution.py:58
  325.2 0.6 compare_reduce_fusion
  325.8 0.7 fusion.13
  326.5 10.0 %custom-call.9 = f32[1,128,128]{1,2,0:T(8,128)S(1)} custom-call(f32[1,128,128]{2,1,0:T(8,128)S(1)} %fusion.13), custom_call_target="InvertDiagBlocksLowerTriangular" | custom-call | tf_op jit(solution)/shard_map/jit(_solve_triangular)/triangular_solve | solution.py:59
  336.9 7.4 %fusion.3 = f32[128,4,2,512]{3,0,2,1:T(8,128)S(1)} fusion(f32[4,512,2,512]{3,1,2,0:T(8,128)} %bitcast.159, f32[128,512]{1,0:T(8,128)S(1)} %fusion.5), kind=kOutput, calls=%fused_computation.6 | convolution fusion | flops 3221225472 | bytes 10747904 | tf_op jit(solution)/shard_map/xr,sxyz->rsyz/dot_general | solution.py:60
  344.3 2.9 copy.55
  347.3 3.6 all-to-all-start.1
  350.9 0.8 copy.57
  351.7 24.8 %all-to-all-done.1 = f32[128,4,2,512]{3,2,1,0:T(2,128)S(1)} async-done(((f32[128,4,2,512]{3,2,1,0:T(2,128)}), f32[128,4,2,512]{3,2,1,0:T(2,128)S(1)}, u32[]{:S(2)}, u32[]{:S(2)}) %all-to-all-start.1) | async-done | bytes 2097184 | tf_op jit(solution)/shard_map/all_to_all | solution.py:67
  376.5 2.5 copy.56
  379.0 3.6 all_to_all.33
  (39 shorter events, 2.7 us)
Async XLA Ops:
  7.2 254.4 %copy-start = (f32[512,128]{1,0:T(8,128)S(1)}, f32[512,128]{1,0:T(8,128)}, u32[]{:S(2)}) copy-start(f32[512,128]{1,0:T(8,128)} %param.6) | copy-start | bytes 786436
  7.2 252.3 %all-reduce.2.cloned.1.call-start = ((), (), s32[]{:S(2)}) async-start(), calls=%async_computation.2 | async-start | bytes 1310720 | tf_op jit(solution)/shard_map/psum | solution.py:48
  112.6 15.4 %copy-start.1 = (f32[4,128,8,512]{3,1,0,2:T(8,128)}, f32[4,128,8,512]{3,1,0,2:T(8,128)S(1)}, u32[]{:S(2)}) copy-start(f32[4,128,8,512]{3,1,0,2:T(8,128)S(1)} %all_to_all.36) | copy-start | bytes 25165828
  128.3 0.8 copy-start.2
  347.3 29.2 %all-to-all-start.1 = ((f32[128,4,2,512]{3,2,1,0:T(2,128)}), f32[128,4,2,512]{3,2,1,0:T(2,128)S(1)}, u32[]{:S(2)}, u32[]{:S(2)}) async-start(f32[128,4,2,512]{3,2,1,0:T(2,128)} %copy.55), calls=%async_computation.1 | async-start | bytes 4194304 | tf_op jit(solution)/shard_map/all_to_all | solution.py:67
Sparse Core Ops, SparseCore 0:
  129.3 130.1 all-reduce.1
where the time goes:
time: 396 us; the launch traced here: 390 us
  waiting for transfers between devices  147 us (37%)
  blocking collectives  97.1 us (25%)
  other arithmetic  69.1 us (17%)
  local copies, waits for them, and re-layouts  29.5 us (7%)
  matrix products  28.8 us (7%)
  between operations  14.8 us (4%)
    psum x1, waiting for transfers between devices, local(): lax.psum(pack_upper(partial_gram), ('wide', 'narrow'))  122 us
    all_to_all x1, blocking collectives, local(): lax.all_to_all(field, 'narrow', split_axis=2, concat_axis=1, tiled=True)  97.1 us
    another operation x9, other arithmetic, local(): lower = jnp.linalg.cholesky(cross)  37.4 us
    another operation x6, other arithmetic, local(): basis = jax.scipy.linalg.solve_triangular(lower, product.T, lower=True).T  31.6 us
    all_to_all x1, waiting for transfers between devices, local(): lax.all_to_all(projected, 'narrow', split_axis=0, concat_axis=2, tiled=True)  24.8 us
    dot_general x1, matrix products, local(): jnp.einsum('sxyz,swyz->xw', regrouped, regrouped, preferred_element_type=...  15.4 us
    unnamed x20, local copies, waits for them, and re-layouts  10.3 us
    all_to_all x1, local copies, waits for them, and re-layouts, local(): lax.all_to_all(field, 'narrow', split_axis=2, concat_axis=1, tiled=True)  8.18 us
  transfers between devices with their start and end apart: 2, of which 2 were waited for; matrix products, arithmetic and copies ran while one was open for 2% of the time, Pallas kernels for 0%

commit v1 on v0

v1 whole, which is shorter than its diff:
```python
import functools

import jax
import jax.numpy as jnp
from jax import lax
from jax.experimental import pallas as pl
from jax.experimental.pallas import tpu as pltpu
from jax.sharding import PartitionSpec as P

ITERS = 3
MESH = pl.DeviceIdType.MESH
LANES = 128
SUB = 8
NT = (((1,), (1,)), ((), ()))
NN = (((1,), (0,)), ((), ()))


def bits_of(size):
    assert size & (size - 1) == 0
    return size.bit_length() - 1


def flip(index, bit):
    step = 2**bit
    mine = lax.rem(index // step, 2)
    return mine, index + (1 - 2 * mine) * step


def other_of(me, shift, groups):
    return lax.rem(me + shift, groups)


def split(value):
    high = value.astype(jnp.bfloat16)
    low = (value - high.astype(jnp.float32)).astype(jnp.bfloat16)
    return high, low


def gram_kernel(groups, wides, chunks, columns, field, saved, gram, buf, main, cross, packed, landed, full,
                send_sem, recv_sem, own_sem, save_sem, red_send, red_recv):
    me = lax.axis_index("narrow")
    wide = lax.axis_index("wide")
    rows = field.shape[1]
    order = main.shape[0]
    block = order // 4
    shifts = [groups // 2] + [s for s in range(1, groups) if s != groups // 2]
    narrow_bits, wide_bits = bits_of(groups), bits_of(wides)

    barrier = pltpu.get_barrier_semaphore()
    for shift in shifts:
        pl.semaphore_signal(barrier, inc=1, device_id={"narrow": other_of(me, shift, groups)}, device_id_type=MESH)
    for bit in range(wide_bits):
        pl.semaphore_signal(barrier, inc=1, device_id={"wide": flip(wide, bit)[1]}, device_id_type=MESH)
    for c in range(chunks):
        pltpu.make_async_copy(
            field.at[me, :, pl.ds(c * LANES, LANES)], buf.at[c, pl.ds(me * rows, rows)], own_sem.at[c]
        ).start()
    pl.semaphore_wait(barrier, groups - 1 + wide_bits)

    def send(c, shift):
        to = other_of(me, shift, groups)
        return pltpu.make_async_remote_copy(
            src_ref=field.at[to, :, pl.ds(c * LANES, LANES)],
            dst_ref=buf.at[c, pl.ds(me * rows, rows)],
            send_sem=send_sem.at[c, shift],
            recv_sem=recv_sem.at[c, shift],
            device_id={"narrow": to},
            device_id_type=MESH,
        )

    for c in range(chunks):
        for shift in shifts:
            send(c, shift).start()
    main[...] = jnp.zeros_like(main)
    cross[...] = jnp.zeros_like(cross)

    for c in range(chunks):
        pltpu.make_async_copy(
            field.at[me, :, pl.ds(c * LANES, LANES)], buf.at[c, pl.ds(me * rows, rows)], own_sem.at[c]
        ).wait()
        for shift in shifts:
            send(c, shift).wait_recv()
        pltpu.make_async_copy(buf.at[c], saved.at[c], save_sem.at[c]).start()

        def pair(q, carry):
            value = jnp.concatenate(
                [buf[c, pl.ds(2 * q + k, order, stride=SUB), :] for k in range(2)], axis=1
            )
            high, low = split(value)
            main[...] += lax.dot_general(high, high, NT, preferred_element_type=jnp.float32)
            cross[...] += lax.dot_general(high, low, NT, preferred_element_type=jnp.float32)
            return carry

        lax.fori_loop(0, SUB // 2, pair, 0)

    pairs = [(i, j) for i in range(4) for j in range(4) if i <= j]
    for place, (i, j) in enumerate(pairs):
        at_i, at_j = pl.ds(i * block, block), pl.ds(j * block, block)
        packed[pl.ds(place * block, block), :] = main[at_i, at_j] + cross[at_i, at_j] + cross[at_j, at_i].T

    size = len(pairs) * block
    low_row = 0
    steps = [("narrow", me, b) for b in range(narrow_bits)] + [("wide", wide, b) for b in range(wide_bits)]
    halved = []
    at = 0
    for place, (axis, index, bit) in enumerate(steps):
        mine, partner = flip(index, bit)
        halve = axis == "narrow" or bit == 0
        if halve:
            size //= 2
            away = low_row + (1 - mine) * size
            low_row = low_row + mine * size
            halved.append((place, axis, partner, size, low_row, away))
        else:
            away = low_row
        copy = pltpu.make_async_remote_copy(
            src_ref=packed.at[pl.ds(pl.multiple_of(away, SUB), size)],
            dst_ref=landed.at[pl.ds(at, size)],
            send_sem=red_send.at[place],
            recv_sem=red_recv.at[place],
            device_id={axis: partner},
            device_id_type=MESH,
        )
        copy.start()
        copy.wait()
        keep = pl.ds(pl.multiple_of(low_row, SUB), size)
        packed[keep, :] = packed[keep, :] + landed[pl.ds(at, size), :]
        at += size
    place = len(steps)
    keep = pl.ds(pl.multiple_of(low_row, SUB), size)
    full[keep, :] = packed[keep, :]
    for _, axis, partner, size, start, away in reversed(halved):
        region = full.at[pl.ds(pl.multiple_of(start, SUB), size)]
        copy = pltpu.make_async_remote_copy(
            src_ref=region,
            dst_ref=region,
            send_sem=red_send.at[place],
            recv_sem=red_recv.at[place],
            device_id={axis: partner},
            device_id_type=MESH,
        )
        copy.start()
        copy.wait()
        place += 1

    scale = 1.0 / columns
    for place, (i, j) in enumerate(pairs):
        at_i, at_j = pl.ds(i * block, block), pl.ds(j * block, block)
        tile = full[pl.ds(place * block, block), :] * scale
        gram[at_i, at_j] = tile
        if i != j:
            gram[at_j, at_i] = tile.T
    for c in range(chunks):
        pltpu.make_async_copy(buf.at[c], saved.at[c], save_sem.at[c]).wait()
        for shift in shifts:
            send(c, shift).wait_send()


def gram_of(field, groups, wides):
    species, rows, cols_y, cells_z = field.shape
    assert species == groups and cols_y == SUB and cells_z % LANES == 0
    order = rows * groups
    chunks = cells_z // LANES
    columns = species * cols_y * wides * cells_z
    total = 10 * (order // 4)
    narrow_bits, wide_bits = bits_of(groups), bits_of(wides)
    flat = field.reshape(species, rows * cols_y, cells_z)
    number = 2 * narrow_bits + wide_bits + 1
    return pl.pallas_call(
        functools.partial(gram_kernel, groups, wides, chunks, columns),
        out_shape=(
            jax.ShapeDtypeStruct((chunks, order * cols_y, LANES), jnp.float32),
            jax.ShapeDtypeStruct((order, order), jnp.float32),
        ),
        in_specs=[pl.BlockSpec(memory_space=pl.ANY)],
        out_specs=(pl.BlockSpec(memory_space=pl.ANY), pl.BlockSpec(memory_space=pltpu.VMEM)),
        scratch_shapes=[
            pltpu.VMEM((chunks, order * cols_y, LANES), jnp.float32),
            pltpu.VMEM((order, order), jnp.float32),
            pltpu.VMEM((order, order), jnp.float32),
            pltpu.VMEM((total, order // 4), jnp.float32),
            pltpu.VMEM((2 * total, order // 4), jnp.float32),
            pltpu.VMEM((total, order // 4), jnp.float32),
            pltpu.SemaphoreType.DMA((chunks, groups)),
            pltpu.SemaphoreType.DMA((chunks, groups)),
            pltpu.SemaphoreType.DMA((chunks,)),
            pltpu.SemaphoreType.DMA((chunks,)),
            pltpu.SemaphoreType.DMA((number,)),
            pltpu.SemaphoreType.DMA((number,)),
        ],
        compiler_params=pltpu.CompilerParams(collective_id=0, has_side_effects=True, vmem_limit_bytes=48 * 2**20),
        name="exchange_gram",
    )(flat)


def lane(tile, k):
    return jnp.broadcast_to(tile[:, k : k + 1], tile.shape)


def sublane(tile, j):
    return jnp.broadcast_to(tile[j : j + 1, :], tile.shape)


def basis_kernel(gram, start, basis, basis_t, work):
    rank = start.shape[1]
    blocks = rank // SUB
    row_id = lax.broadcasted_iota(jnp.int32, (SUB, rank), 0)
    high = lax.Precision.HIGHEST

    def dot(a, b, dims):
        return lax.dot_general(a, b, dims, precision=high, preferred_element_type=jnp.float32)

    def step(_, carry):
        product = dot(basis_t[...], gram[...], NN)
        work[:, :rank] = dot(product, product, NT)
        eye = lax.broadcasted_iota(jnp.int32, (rank, rank), 0) == lax.broadcasted_iota(jnp.int32, (rank, rank), 1)
        work[:, rank:] = eye.astype(jnp.float32)
        for b in range(blocks):
            here = pl.ds(b * SUB, SUB)
            left, right = work[here, :rank], work[here, rank:]
            cols = [lane(left, b * SUB + k) for k in range(SUB)]
            scales, lefts, rights, coefs = [], [], [], []
            for j in range(SUB):
                inverse = lax.rsqrt(sublane(cols[j], j))
                u_left, u_right = sublane(left, j) * inverse, sublane(right, j) * inverse
                coef = {k: sublane(cols[k], j) * inverse for k in range(j + 1, SUB)}
                mult = jnp.where(row_id > j, cols[j] * inverse, 0.0)
                for k in range(j + 1, SUB):
                    cols[k] = cols[k] - mult * coef[k]
                left = left - mult * u_left
                right = jnp.where(row_id == j, u_right, right - mult * u_right)
                scales.append(inverse)
                lefts.append(u_left)
                rights.append(u_right)
                coefs.append(coef)
            work[here, rank:] = right
            for g in range(b + 1, blocks):
                there = pl.ds(g * SUB, SUB)
                left, right = work[there, :rank], work[there, rank:]
                cols = [lane(left, b * SUB + k) for k in range(SUB)]
                for j in range(SUB):
                    mult = cols[j] * scales[j]
                    for k in range(j + 1, SUB):
                        cols[k] = cols[k] - mult * coefs[j][k]
                    left = left - mult * lefts[j]
                    right = right - mult * rights[j]
                work[there, :rank] = left
                work[there, rank:] = right
        basis_t[...] = dot(work[:, rank:], product, NN)
        return carry

    basis_t[...] = start[...].T
    lax.fori_loop(0, ITERS, step, 0)
    basis[...] = basis_t[...].T


def basis_of(gram, start):
    order, rank = start.shape
    return pl.pallas_call(
        basis_kernel,
        out_shape=(
            jax.ShapeDtypeStruct((order, rank), jnp.float32),
            jax.ShapeDtypeStruct((rank, order), jnp.float32),
        ),
        in_specs=[pl.BlockSpec(memory_space=pltpu.VMEM)] * 2,
        out_specs=(pl.BlockSpec(memory_space=pltpu.VMEM),) * 2,
        scratch_shapes=[pltpu.VMEM((rank, 2 * rank), jnp.float32)],
        compiler_params=pltpu.CompilerParams(vmem_limit_bytes=48 * 2**20),
        name="iterate_basis",
    )(gram, start)


def core_kernel(groups, chunks, basis_t, saved, core, buf, stage, load_sem, send_sem, recv_sem, own_sem):
    me = lax.axis_index("narrow")
    rank, order = basis_t.shape
    share = rank // groups
    shifts = [groups // 2] + [s for s in range(1, groups) if s != groups // 2]
    for c in range(chunks):
        pltpu.make_async_copy(saved.at[c], buf.at[c], load_sem.at[c]).start()
    barrier = pltpu.get_barrier_semaphore()
    for shift in shifts:
        pl.semaphore_signal(barrier, inc=1, device_id={"narrow": other_of(me, shift, groups)}, device_id_type=MESH)
    left = jnp.concatenate(split(basis_t[...]), axis=0)
    pl.semaphore_wait(barrier, groups - 1)

    def target(c):
        return core.at[:, pl.ds(me * SUB, SUB), pl.ds(c * LANES, LANES)]

    def send(c, shift):
        to = other_of(me, shift, groups)
        return pltpu.make_async_remote_copy(
            src_ref=stage.at[c, pl.ds(to * share, share)],
            dst_ref=target(c),
            send_sem=send_sem.at[c, shift],
            recv_sem=recv_sem.at[c, shift],
            device_id={"narrow": to},
            device_id_type=MESH,
        )

    def own(c):
        return pltpu.make_async_copy(stage.at[c, pl.ds(me * share, share)], target(c), own_sem.at[c])

    for c in range(chunks):
        pltpu.make_async_copy(saved.at[c], buf.at[c], load_sem.at[c]).wait()
        flat = stage.at[c].reshape(rank * SUB, LANES)
        for q in range(SUB // 2):
            value = jnp.concatenate(
                [buf[c, pl.ds(2 * q + k, order, stride=SUB), :] for k in range(2)], axis=1
            )
            high, low = split(value)
            both = lax.dot_general(left, high, NN, preferred_element_type=jnp.float32)
            rest = lax.dot_general(left[:rank], low, NN, preferred_element_type=jnp.float32)
            out = both[:rank] + (both[rank:] + rest)
            for k in range(2):
                flat[pl.ds(2 * q + k, rank, stride=SUB), :] = out[:, k * LANES : (k + 1) * LANES]
        for shift in shifts:
            send(c, shift).start()
        own(c).start()
    for c in range(chunks):
        own(c).wait()
        for shift in shifts:
            send(c, shift).wait()


def core_of(basis_t, saved, shape, groups):
    species, rows, cols_y, cells_z = shape
    rank, order = basis_t.shape
    chunks = cells_z // LANES
    core = pl.pallas_call(
        functools.partial(core_kernel, groups, chunks),
        out_shape=jax.ShapeDtypeStruct((rank // groups, species * cols_y, cells_z), jnp.float32),
        in_specs=[pl.BlockSpec(memory_space=pltpu.VMEM), pl.BlockSpec(memory_space=pl.ANY)],
        out_specs=pl.BlockSpec(memory_space=pl.ANY),
        scratch_shapes=[
            pltpu.VMEM(saved.shape, jnp.float32),
            pltpu.VMEM((chunks, rank, cols_y, LANES), jnp.float32),
            pltpu.SemaphoreType.DMA((chunks,)),
            pltpu.SemaphoreType.DMA((chunks, groups)),
            pltpu.SemaphoreType.DMA((chunks, groups)),
            pltpu.SemaphoreType.DMA((chunks,)),
        ],
        compiler_params=pltpu.CompilerParams(collective_id=1, has_side_effects=True, vmem_limit_bytes=48 * 2**20),
        name="project_core",
    )(basis_t, saved)
    return core.reshape(rank // groups, species, cols_y, cells_z)


def local(field, start):
    groups, wides = lax.axis_size("narrow"), lax.axis_size("wide")
    saved, gram = gram_of(field, groups, wides)
    basis, basis_t = basis_of(gram, start)
    return basis, core_of(basis_t, saved, field.shape, groups)


def solution(mesh):
    return jax.shard_map(
        local,
        mesh=mesh,
        in_specs=(P(None, "narrow", "wide", None), P()),
        out_specs=(P(), P("narrow", None, "wide", None)),
        check_vma=False,
    )
```

time: 396 us -> 175 us (0.44); the launches traced: 390 us -> 175 us
  Pallas kernels: 0 us -> 173 us
  waiting for transfers between devices: 147 us -> 0 us
  blocking collectives: 97.1 us -> 0 us
  other arithmetic: 69.1 us -> 0 us
  matrix products: 28.8 us -> 0 us
  local copies, waits for them, and re-layouts: 29.5 us -> 1.33 us
  between operations: 14.8 us -> 0.66 us
    pallas_call x0 -> x3, Pallas kernels: none -> 173 us  [the longest x1 127 us: gram_of(): pl.pallas_call(functools.partial(gram_kernel, groups, wides, chunks, colu...]
    psum x1 -> x0, waiting for transfers between devices: 122 us -> none  [local(): lax.psum(pack_upper(partial_gram), ('wide', 'narrow'))]
    all_to_all x1 -> x0, blocking collectives: 97.1 us -> none  [local(): lax.all_to_all(field, 'narrow', split_axis=2, concat_axis=1, tiled=True)]
    another operation x15 -> x0, other arithmetic: 69 us -> none  [the longest x9 37.4 us: local(): lower = jnp.linalg.cholesky(cross)]
    dot_general x8 -> x0, matrix products: 27.5 us -> none  [the longest x1 15.4 us: local(): jnp.einsum('sxyz,swyz->xw', regrouped, regrouped, preferred_element_type=...]
    all_to_all x1 -> x0, waiting for transfers between devices: 24.8 us -> none  [local(): lax.all_to_all(projected, 'narrow', split_axis=0, concat_axis=2, tiled=True)]
    all_to_all x3 -> x0, local copies, waits for them, and re-layouts: 14.3 us -> none  [the longest x1 8.18 us: local(): lax.all_to_all(field, 'narrow', split_axis=2, concat_axis=1, tiled=True)]
    unnamed x20 -> x3, local copies, waits for them, and re-layouts: 10.3 us -> 1.33 us
  transfers between devices with their start and end apart: 2 -> 0, of which waited for: 2 -> 0; matrix products, arithmetic and copies ran while one was open for 2% -> 0% of each run, Pallas kernels for 0% -> 0%
where the time goes in v1:
time: 175 us
  Pallas kernels  173 us (99%)
    pallas_call x1, Pallas kernels, gram_of(): pl.pallas_call(functools.partial(gram_kernel, groups, wides, chunks, colu...  127 us
    pallas_call x1, Pallas kernels, core_of(): pl.pallas_call(functools.partial(core_kernel, groups, chunks), out_shape=...  28 us
    pallas_call x1, Pallas kernels, basis_of(): pl.pallas_call(basis_kernel, out_shape=(jax.ShapeDtypeStruct((order, rank...  18.3 us

profile of v1, /device:TPU:0, one launch (start us, length us, event | category | flops | bytes accessed | tf_op | source)
XLA Modules:
  0.0 175.2 jit_solution(8446349559297888035)
XLA Ops:
  0.6 0.0 copy-start
  0.6 126.9 %exchange_gram.1 = (f32[4,4096,128]{2,1,0:T(8,128)}, f32[512,512]{1,0:T(8,128)S(1)}) custom-call(f32[4,1024,512]{2,1,0:T(8,128)} %bitcast.3), custom_call_target="tpu_custom_call" | custom-call | tf_op jit(solution)/shard_map/exchange_gram/pallas_call | solution.py:169
  127.5 0.0 copy-done
  127.5 18.3 %iterate_basis.1 = (f32[512,128]{1,0:T(8,128)}, f32[128,512]{1,0:T(8,128)S(1)}) custom-call(f32[512,512]{1,0:T(8,128)S(1)} %get-tuple-element.6.gram, f32[512,128]{1,0:T(8,128)S(1)} %copy-done), custom_call_target="tpu_custom_call" | custom-call | tf_op jit(solution)/shard_map/iterate_basis/pallas_call | solution.py:259
  145.8 28.0 %project_core.1 = f32[32,32,512]{2,1,0:T(8,128)S(1)} custom-call(f32[128,512]{1,0:T(8,128)S(1)} %get-tuple-element.8.basis_t, f32[4,4096,128]{2,1,0:T(8,128)} %get-tuple-element.9.saved), custom_call_target="tpu_custom_call" | custom-call | tf_op jit(solution)/shard_map/project_core/pallas_call | solution.py:329
  173.9 1.3 copy.5
Async XLA Ops:
  0.6 126.9 %copy-start = (f32[512,128]{1,0:T(8,128)S(1)}, f32[512,128]{1,0:T(8,128)}, u32[]{:S(2)}) copy-start(f32[512,128]{1,0:T(8,128)} %start.1) | copy-start | bytes 786436

commit v2 on v1

--- a/solution.py
+++ b/solution.py
@@ -94,62 +94,85 @@
         lax.fori_loop(0, SUB // 2, pair, 0)
 
     pairs = [(i, j) for i in range(4) for j in range(4) if i <= j]
-    for place, (i, j) in enumerate(pairs):
-        at_i, at_j = pl.ds(i * block, block), pl.ds(j * block, block)
-        packed[pl.ds(place * block, block), :] = main[at_i, at_j] + cross[at_i, at_j] + cross[at_j, at_i].T
-
-    size = len(pairs) * block
-    low_row = 0
-    steps = [("narrow", me, b) for b in range(narrow_bits)] + [("wide", wide, b) for b in range(wide_bits)]
-    halved = []
-    at = 0
-    for place, (axis, index, bit) in enumerate(steps):
-        mine, partner = flip(index, bit)
-        halve = axis == "narrow" or bit == 0
-        if halve:
-            size //= 2
-            away = low_row + (1 - mine) * size
-            low_row = low_row + mine * size
-            halved.append((place, axis, partner, size, low_row, away))
-        else:
-            away = low_row
-        copy = pltpu.make_async_remote_copy(
-            src_ref=packed.at[pl.ds(pl.multiple_of(away, SUB), size)],
-            dst_ref=landed.at[pl.ds(at, size)],
-            send_sem=red_send.at[place],
-            recv_sem=red_recv.at[place],
+    scale = 1.0 / columns
+    total = len(pairs) * block // 2
+    index = {"narrow": me, "wide": wide}
+    halving = [("narrow", b) for b in range(narrow_bits)] + [("wide", 0)]
+    whole = [("wide", b) for b in range(1, wide_bits)]
+    number = 2 * len(halving) + len(whole)
+    room = landed.shape[0] // 2
+
+    def rows_at(start, size):
+        return pl.ds(pl.multiple_of(start, SUB), size)
+
+    def remote(source, target, sem, axis, partner):
+        return pltpu.make_async_remote_copy(
+            src_ref=source,
+            dst_ref=target,
+            send_sem=red_send.at[sem],
+            recv_sem=red_recv.at[sem],
             device_id={axis: partner},
             device_id_type=MESH,
         )
-        copy.start()
-        copy.wait()
-        keep = pl.ds(pl.multiple_of(low_row, SUB), size)
-        packed[keep, :] = packed[keep, :] + landed[pl.ds(at, size), :]
-        at += size
-    place = len(steps)
-    keep = pl.ds(pl.multiple_of(low_row, SUB), size)
-    full[keep, :] = packed[keep, :]
-    for _, axis, partner, size, start, away in reversed(halved):
-        region = full.at[pl.ds(pl.multiple_of(start, SUB), size)]
-        copy = pltpu.make_async_remote_copy(
-            src_ref=region,
-            dst_ref=region,
-            send_sem=red_send.at[place],
-            recv_sem=red_recv.at[place],
-            device_id={axis: partner},
-            device_id_type=MESH,
-        )
-        copy.start()
-        copy.wait()
-        place += 1
-
-    scale = 1.0 / columns
-    for place, (i, j) in enumerate(pairs):
-        at_i, at_j = pl.ds(i * block, block), pl.ds(j * block, block)
-        tile = full[pl.ds(place * block, block), :] * scale
-        gram[at_i, at_j] = tile
-        if i != j:
-            gram[at_j, at_i] = tile.T
+
+    def chain(half, halves, wholes):
+        size, low_row, at, sem = total, half * total, half * room, half * number
+        steps, back = [], []
+        for place, (axis, bit) in enumerate(halves + wholes):
+            mine, partner = flip(index[axis], bit)
+            away = low_row
+            if place < len(halves):
+                size //= 2
+                away = low_row + (1 - mine) * size
+                low_row = low_row + mine * size
+                back.append((axis, partner, low_row, size))
+            target = full if place == len(halves) + len(wholes) - 1 else packed
+            here = pl.ds(at, size)
+            copy = remote(packed.at[rows_at(away, size)], landed.at[here], sem, axis, partner)
+
+            def finish(keep=rows_at(low_row, size), here=here, target=target):
+                target[keep, :] = packed[keep, :] + landed[here, :]
+
+            steps.append((copy, finish))
+            at, sem = at + size, sem + 1
+        for axis, partner, start, size in reversed(back):
+            region = full.at[rows_at(start, size)]
+            steps.append((remote(region, region, sem, axis, partner), None))
+            sem += 1
+        return steps
+
+    def pack(half):
+        for place, (i, j) in enumerate(pairs):
+            if place // (len(pairs) // 2) == half:
+                at_i, at_j = pl.ds(i * block, block), pl.ds(j * block, block)
+                packed[pl.ds(place * block, block), :] = main[at_i, at_j] + cross[at_i, at_j] + cross[at_j, at_i].T
+
+    def unpack(half):
+        for place, (i, j) in enumerate(pairs):
+            if place // (len(pairs) // 2) == half:
+                at_i, at_j = pl.ds(i * block, block), pl.ds(j * block, block)
+                tile = full[pl.ds(place * block, block), :] * scale
+                gram[at_i, at_j] = tile
+                if i != j:
+                    gram[at_j, at_i] = tile.T
+
+    chains = [
+        chain(0, halving, whole),
+        chain(1, halving[:1] + halving[:0:-1], whole[::-1]),
+    ]
+    for half in range(2):
+        pack(half)
+        chains[half][0][0].start()
+    for place in range(number):
+        for half in range(2):
+            copy, finish = chains[half][place]
+            copy.wait()
+            if finish is not None:
+                finish()
+            if place + 1 < number:
+                chains[half][place + 1][0].start()
+            else:
+                unpack(half)
     for c in range(chunks):
         pltpu.make_async_copy(buf.at[c], saved.at[c], save_sem.at[c]).wait()
         for shift in shifts:
@@ -165,7 +188,7 @@
     total = 10 * (order // 4)
     narrow_bits, wide_bits = bits_of(groups), bits_of(wides)
     flat = field.reshape(species, rows * cols_y, cells_z)
-    number = 2 * narrow_bits + wide_bits + 1
+    number = 2 * (2 * narrow_bits + wide_bits + 1)
     return pl.pallas_call(
         functools.partial(gram_kernel, groups, wides, chunks, columns),
         out_shape=(

time: 175 us -> 170 us (0.971)
  Pallas kernels: 173 us -> 168 us
    pallas_call x1, Pallas kernels: 127 us -> 122 us  [gram_of(): pl.pallas_call(functools.partial(gram_kernel, groups, wides, chunks, colu...]
where the time goes in v2:
time: 170 us
  Pallas kernels  168 us (99%)
    pallas_call x1, Pallas kernels, gram_of(): pl.pallas_call(functools.partial(gram_kernel, groups, wides, chunks, colu...  122 us
    pallas_call x1, Pallas kernels, core_of(): pl.pallas_call(functools.partial(core_kernel, groups, chunks), out_shape=...  27 us
    pallas_call x1, Pallas kernels, basis_of(): pl.pallas_call(basis_kernel, out_shape=(jax.ShapeDtypeStruct((order, rank...  18.3 us

profile of v2, /device:TPU:0, one launch (start us, length us, event | category | flops | bytes accessed | tf_op | source)
XLA Modules:
  0.0 169.5 jit_solution(12287934692798413388)
XLA Ops:
  0.6 0.0 copy-start
  0.6 122.3 %exchange_gram.1 = (f32[4,4096,128]{2,1,0:T(8,128)}, f32[512,512]{1,0:T(8,128)S(1)}) custom-call(f32[4,1024,512]{2,1,0:T(8,128)} %bitcast.3), custom_call_target="tpu_custom_call" | custom-call | tf_op jit(solution)/shard_map/exchange_gram/pallas_call | solution.py:192
  122.9 0.0 copy-done
  122.9 18.3 %iterate_basis.1 = (f32[512,128]{1,0:T(8,128)}, f32[128,512]{1,0:T(8,128)S(1)}) custom-call(f32[512,512]{1,0:T(8,128)S(1)} %get-tuple-element.6.gram, f32[512,128]{1,0:T(8,128)S(1)} %copy-done), custom_call_target="tpu_custom_call" | custom-call | tf_op jit(solution)/shard_map/iterate_basis/pallas_call | solution.py:282
  141.2 27.0 %project_core.1 = f32[32,32,512]{2,1,0:T(8,128)S(1)} custom-call(f32[128,512]{1,0:T(8,128)S(1)} %get-tuple-element.8.basis_t, f32[4,4096,128]{2,1,0:T(8,128)} %get-tuple-element.9.saved), custom_call_target="tpu_custom_call" | custom-call | tf_op jit(solution)/shard_map/project_core/pallas_call | solution.py:352
  168.2 1.3 copy.5
Async XLA Ops:
  0.6 122.3 %copy-start = (f32[512,128]{1,0:T(8,128)S(1)}, f32[512,128]{1,0:T(8,128)}, u32[]{:S(2)}) copy-start(f32[512,128]{1,0:T(8,128)} %start.1) | copy-start | bytes 786436

commit v3 on v2

--- a/solution.py
+++ b/solution.py
@@ -36,7 +36,7 @@
     return high, low
 
 
-def gram_kernel(groups, wides, chunks, columns, field, saved, gram, buf, main, cross, packed, landed, full,
+def gram_kernel(groups, wides, chunks, columns, field, saved, gram, buf, highs, lows, main, cross, packed, landed, full,
                 send_sem, recv_sem, own_sem, save_sem, red_send, red_recv):
     me = lax.axis_index("narrow")
     wide = lax.axis_index("wide")
@@ -74,24 +74,29 @@
     main[...] = jnp.zeros_like(main)
     cross[...] = jnp.zeros_like(cross)
 
+    share, middle = order // groups, order // 2
+
+    def convert(c, source):
+        there = pl.ds(pl.multiple_of(source * share, share), share)
+        for y in range(SUB):
+            value = buf[c, pl.ds(source * rows + y, share, stride=SUB), :]
+            highs[there, y * LANES : (y + 1) * LANES], lows[there, y * LANES : (y + 1) * LANES] = split(value)
+
+    def product(a, b):
+        return lax.dot_general(a, b, NT, preferred_element_type=jnp.float32)
+
     for c in range(chunks):
         pltpu.make_async_copy(
             field.at[me, :, pl.ds(c * LANES, LANES)], buf.at[c, pl.ds(me * rows, rows)], own_sem.at[c]
         ).wait()
+        convert(c, me)
         for shift in shifts:
             send(c, shift).wait_recv()
+            convert(c, other_of(me, groups - shift, groups))
         pltpu.make_async_copy(buf.at[c], saved.at[c], save_sem.at[c]).start()
-
-        def pair(q, carry):
-            value = jnp.concatenate(
-                [buf[c, pl.ds(2 * q + k, order, stride=SUB), :] for k in range(2)], axis=1
-            )
-            high, low = split(value)
-            main[...] += lax.dot_general(high, high, NT, preferred_element_type=jnp.float32)
-            cross[...] += lax.dot_general(high, low, NT, preferred_element_type=jnp.float32)
-            return carry
-
-        lax.fori_loop(0, SUB // 2, pair, 0)
+        main[:middle, :] += product(highs[:middle, :], highs[...])
+        main[middle:, middle:] += product(highs[middle:, :], highs[middle:, :])
+        cross[...] += product(highs[...], lows[...])
 
     pairs = [(i, j) for i in range(4) for j in range(4) if i <= j]
     scale = 1.0 / columns
@@ -199,6 +204,8 @@
         out_specs=(pl.BlockSpec(memory_space=pl.ANY), pl.BlockSpec(memory_space=pltpu.VMEM)),
         scratch_shapes=[
             pltpu.VMEM((chunks, order * cols_y, LANES), jnp.float32),
+            pltpu.VMEM((order, cols_y * LANES), jnp.bfloat16),
+            pltpu.VMEM((order, cols_y * LANES), jnp.bfloat16),
             pltpu.VMEM((order, order), jnp.float32),
             pltpu.VMEM((order, order), jnp.float32),
             pltpu.VMEM((total, order // 4), jnp.float32),
@@ -304,7 +311,6 @@
     for shift in shifts:
         pl.semaphore_signal(barrier, inc=1, device_id={"narrow": other_of(me, shift, groups)}, device_id_type=MESH)
     left = jnp.concatenate(split(basis_t[...]), axis=0)
-    pl.semaphore_wait(barrier, groups - 1)
 
     def target(c):
         return core.at[:, pl.ds(me * SUB, SUB), pl.ds(c * LANES, LANES)]
@@ -336,6 +342,8 @@
             out = both[:rank] + (both[rank:] + rest)
             for k in range(2):
                 flat[pl.ds(2 * q + k, rank, stride=SUB), :] = out[:, k * LANES : (k + 1) * LANES]
+        if c == 0:
+            pl.semaphore_wait(barrier, groups - 1)
         for shift in shifts:
             send(c, shift).start()
         own(c).start()

time: 170 us -> 169 us (level)
  no operation moved by 1% of the time
where the time goes in v3:
time: 169 us
  Pallas kernels  167 us (99%)
    pallas_call x1, Pallas kernels, gram_of(): pl.pallas_call(functools.partial(gram_kernel, groups, wides, chunks, colu...  122 us
    pallas_call x1, Pallas kernels, core_of(): pl.pallas_call(functools.partial(core_kernel, groups, chunks), out_shape=...  27.1 us
    pallas_call x1, Pallas kernels, basis_of(): pl.pallas_call(basis_kernel, out_shape=(jax.ShapeDtypeStruct((order, rank...  18.5 us

profile of v3, /device:TPU:0, one launch (start us, length us, event | category | flops | bytes accessed | tf_op | source)
XLA Modules:
  0.0 169.2 jit_solution(16604220328773616942)
XLA Ops:
  0.6 0.0 copy-start
  0.6 121.6 %exchange_gram.1 = (f32[4,4096,128]{2,1,0:T(8,128)}, f32[512,512]{1,0:T(8,128)S(1)}) custom-call(f32[4,1024,512]{2,1,0:T(8,128)} %bitcast.3), custom_call_target="tpu_custom_call" | custom-call | tf_op jit(solution)/shard_map/exchange_gram/pallas_call | solution.py:197
  122.2 0.0 copy-done
  122.2 18.5 %iterate_basis.1 = (f32[512,128]{1,0:T(8,128)}, f32[128,512]{1,0:T(8,128)S(1)}) custom-call(f32[512,512]{1,0:T(8,128)S(1)} %get-tuple-element.6.gram, f32[512,128]{1,0:T(8,128)S(1)} %copy-done), custom_call_target="tpu_custom_call" | custom-call | tf_op jit(solution)/shard_map/iterate_basis/pallas_call | solution.py:289
  140.7 27.1 %project_core.1 = f32[32,32,512]{2,1,0:T(8,128)S(1)} custom-call(f32[128,512]{1,0:T(8,128)S(1)} %get-tuple-element.8.basis_t, f32[4,4096,128]{2,1,0:T(8,128)} %get-tuple-element.9.saved), custom_call_target="tpu_custom_call" | custom-call | tf_op jit(solution)/shard_map/project_core/pallas_call | solution.py:360
  167.8 1.3 copy.5
Async XLA Ops:
  0.6 121.6 %copy-start = (f32[512,128]{1,0:T(8,128)S(1)}, f32[512,128]{1,0:T(8,128)}, u32[]{:S(2)}) copy-start(f32[512,128]{1,0:T(8,128)} %start.1) | copy-start | bytes 786436

commit v4 on v3

--- a/solution.py
+++ b/solution.py
@@ -231,7 +231,7 @@
     return jnp.broadcast_to(tile[j : j + 1, :], tile.shape)
 
 
-def basis_kernel(gram, start, basis, basis_t, work):
+def basis_kernel(gram, start, basis, basis_t, work, gram_high, gram_low):
     rank = start.shape[1]
     blocks = rank // SUB
     row_id = lax.broadcasted_iota(jnp.int32, (SUB, rank), 0)
@@ -241,7 +241,10 @@
         return lax.dot_general(a, b, dims, precision=high, preferred_element_type=jnp.float32)
 
     def step(_, carry):
-        product = dot(basis_t[...], gram[...], NN)
+        parts = jnp.concatenate(split(basis_t[...]), axis=0)
+        both = lax.dot_general(parts, gram_high[...], NN, preferred_element_type=jnp.float32)
+        rest = lax.dot_general(parts[:rank], gram_low[...], NN, preferred_element_type=jnp.float32)
+        product = both[:rank] + (both[rank:] + rest)
         work[:, :rank] = dot(product, product, NT)
         eye = lax.broadcasted_iota(jnp.int32, (rank, rank), 0) == lax.broadcasted_iota(jnp.int32, (rank, rank), 1)
         work[:, rank:] = eye.astype(jnp.float32)
@@ -280,6 +283,7 @@
         return carry
 
     basis_t[...] = start[...].T
+    gram_high[...], gram_low[...] = split(gram[...])
     lax.fori_loop(0, ITERS, step, 0)
     basis[...] = basis_t[...].T
 
@@ -294,7 +298,11 @@
         ),
         in_specs=[pl.BlockSpec(memory_space=pltpu.VMEM)] * 2,
         out_specs=(pl.BlockSpec(memory_space=pltpu.VMEM),) * 2,
-        scratch_shapes=[pltpu.VMEM((rank, 2 * rank), jnp.float32)],
+        scratch_shapes=[
+            pltpu.VMEM((rank, 2 * rank), jnp.float32),
+            pltpu.VMEM((order, order), jnp.bfloat16),
+            pltpu.VMEM((order, order), jnp.bfloat16),
+        ],
         compiler_params=pltpu.CompilerParams(vmem_limit_bytes=48 * 2**20),
         name="iterate_basis",
     )(gram, start)

time: 169 us -> 169 us (level)
  no operation moved by 1% of the time
where the time goes in v4:
time: 169 us; the launch traced here: 168 us
  Pallas kernels  166 us (98%)
    pallas_call x1, Pallas kernels, gram_of(): pl.pallas_call(functools.partial(gram_kernel, groups, wides, chunks, colu...  122 us
    pallas_call x1, Pallas kernels, core_of(): pl.pallas_call(functools.partial(core_kernel, groups, chunks), out_shape=...  27.1 us
    pallas_call x1, Pallas kernels, basis_of(): pl.pallas_call(basis_kernel, out_shape=(jax.ShapeDtypeStruct((order, rank...  17.8 us

profile of v4, /device:TPU:0, one launch (start us, length us, event | category | flops | bytes accessed | tf_op | source)
XLA Modules:
  0.0 168.5 jit_solution(11313706017138637398)
XLA Ops:
  0.6 0.0 copy-start
  0.6 121.6 %exchange_gram.1 = (f32[4,4096,128]{2,1,0:T(8,128)}, f32[512,512]{1,0:T(8,128)S(1)}) custom-call(f32[4,1024,512]{2,1,0:T(8,128)} %bitcast.3), custom_call_target="tpu_custom_call" | custom-call | tf_op jit(solution)/shard_map/exchange_gram/pallas_call | solution.py:197
  122.2 0.0 copy-done
  122.2 17.8 %iterate_basis.1 = (f32[512,128]{1,0:T(8,128)}, f32[128,512]{1,0:T(8,128)S(1)}) custom-call(f32[512,512]{1,0:T(8,128)S(1)} %get-tuple-element.6.gram, f32[512,128]{1,0:T(8,128)S(1)} %copy-done), custom_call_target="tpu_custom_call" | custom-call | tf_op jit(solution)/shard_map/iterate_basis/pallas_call | solution.py:293
  140.0 27.1 %project_core.1 = f32[32,32,512]{2,1,0:T(8,128)S(1)} custom-call(f32[128,512]{1,0:T(8,128)S(1)} %get-tuple-element.8.basis_t, f32[4,4096,128]{2,1,0:T(8,128)} %get-tuple-element.9.saved), custom_call_target="tpu_custom_call" | custom-call | tf_op jit(solution)/shard_map/project_core/pallas_call | solution.py:368
  167.2 1.3 copy.5
Async XLA Ops:
  0.6 121.6 %copy-start = (f32[512,128]{1,0:T(8,128)S(1)}, f32[512,128]{1,0:T(8,128)}, u32[]{:S(2)}) copy-start(f32[512,128]{1,0:T(8,128)} %start.1) | copy-start | bytes 786436
